TPU v7x, 32 devices: a whole 2x2x4 slice. The times are simulated.
32 devices in a mesh: dp: 8 (over z, y), filt: 4 (over x, core).
Axes of the slice: x: 2, y: 2, z: 4, core: 2. Of those that a mesh axis runs over, the one named last changes fastest.
Arguments:
- chars: int32 [8, 512, 50], P('dp'), may hold values from 0 to 261
- lengths: int32 [8], P('dp'), may hold values from 385 to 512, as said below
- char_table: bfloat16 [262, 16], replicated, may hold values from -6 to 6
- conv_weight: bfloat16 [112, 2048], P(None, 'filt'), may hold values from -0.5 to 0.5
- conv_bias: bfloat16 [2048], P('filt'), may hold values from -3 to 3
- highway_weight: bfloat16 [1, 2048, 4096], P(None, 'dp'), may hold values from -0.125 to 0.125
- highway_bias: bfloat16 [1, 4096], P(None, 'dp'), may hold values from -3 to 3
- proj_weight: bfloat16 [2048, 768], P('dp'), may hold values from -0.125 to 0.125
- proj_bias: bfloat16 [768], P('dp'), may hold values from -3 to 3
- position: bfloat16 [512, 768], P('filt'), may hold values from -3 to 3
- norm_gain: bfloat16 [3, 768], P(None, 'dp'), may hold values from 0.099609375 to 1.8984375
- norm_bias: bfloat16 [3, 768], P(None, 'dp'), may hold values from -2 to 2
- query_key_value_weight: bfloat16 [768, 2304], P('dp'), may hold values from -0.21875 to 0.21875
- attention_output_weight: bfloat16 [768, 768], P('dp'), may hold values from -0.875 to 0.875
- feedforward_input_weight: bfloat16 [768, 3072], P('dp'), may hold values from -0.21875 to 0.21875
- feedforward_input_bias: bfloat16 [3072], P('dp'), may hold values from -3 to 3
- feedforward_output_weight: bfloat16 [3072, 768], P('dp'), may hold values from -0.109375 to 0.109375
- cotangent: bfloat16 [8, 512, 768], P('dp', 'filt'), may hold values from -6 to 6
Outputs:
- encoded: bfloat16 [8, 512, 768], P('dp', 'filt')
- grad_char_table: float32 [262, 16], replicated
- grad_conv_weight: float32 [112, 2048], P(None, 'filt')
- grad_conv_bias: float32 [2048], P('filt')
- grad_highway_weight: float32 [1, 2048, 4096], P(None, 'dp')
- grad_highway_bias: float32 [1, 4096], P(None, 'dp')
- grad_proj_weight: float32 [2048, 768], P('dp')
- grad_proj_bias: float32 [768], P('dp')
- grad_position: float32 [512, 768], P('filt')
- grad_norm_gain: float32 [3, 768], P(None, 'dp')
- grad_norm_bias: float32 [3, 768], P(None, 'dp')
- grad_qkv_weight: float32 [768, 2304], P('dp')
- grad_out_weight: float32 [768, 768], P('dp')
- grad_ffn_in_weight: float32 [768, 3072], P('dp')
- grad_ffn_in_bias: float32 [3072], P('dp')
- grad_ffn_out_weight: float32 [3072, 768], P('dp')
Inputs may be any that keep to these rules, and one draw needn't show every extreme that they name: `lengths`: every sequence fills more than three quarters of its 512 slots, and some sequence fills all of them.
All inputs are finite; a program needn't handle non-finite values.
Results may differ from a plain program's by a relative error of at most 0.017.
Values may be sent and summed in bfloat16 or wider, within the bound.
A program may use at most 256 MiB of HBM per device.

v0:
```python
from functools import reduce
import math

import jax
import jax.numpy as jnp
from jax import lax
from jax.sharding import PartitionSpec as P

KW = 7
NF = 2048
HD = 64


eps_norm = 1e-12


def exact_gaussian_activation(values):
    return jax.nn.gelu(values, approximate=False)


def gelu_back(values, upstream):
    return jax.vjp(exact_gaussian_activation, values)[1](upstream)[0]


def layer_norm(values, scale, offset):
    center = values - jnp.mean(values, axis=-1, keepdims=True)
    spread = jnp.mean(center * center, axis=-1, keepdims=True)
    return center * lax.rsqrt(spread + eps_norm) * scale + offset


def channel_widths(channels):
    widths = jnp.ones_like(channels)
    for power in range(6):
        widths = widths + (channels >= NF * 2**power // 64).astype(jnp.int32)
    return widths


def highway_mix(hidden, gates):
    width = hidden.shape[1]
    carry_gate = jax.nn.sigmoid(gates[:, width:])
    return carry_gate * hidden + (1.0 - carry_gate) * exact_gaussian_activation(gates[:, :width])


def char_grid(word_ids, char_table, masked_weight, bias_row, valid):
    vocab = jnp.arange(char_table.shape[0], dtype=jnp.int32)
    onehot = (word_ids[..., None] == vocab).astype(jnp.bfloat16)
    embedded = jnp.einsum(
        "wpv,vd->wpd", onehot, char_table, preferred_element_type=jnp.float32
    ).astype(jnp.bfloat16)
    letters = word_ids.shape[1]
    padded = jnp.pad(embedded, ((0, 0), (0, KW - 1), (0, 0)))
    patches = jnp.concatenate(
        [padded[:, shift_tap : shift_tap + letters, :] for shift_tap in range(KW)], axis=2
    )
    grid = (
        jnp.einsum("wpk,kc->wpc", patches, masked_weight, preferred_element_type=jnp.float32)
        + bias_row
    )
    grid = jnp.where(valid, grid, -1e30)
    row_top = jnp.max(grid, axis=1, keepdims=True)
    log_total = row_top[:, 0, :] + jnp.log(jnp.sum(jnp.exp(grid - row_top), axis=1))
    return (onehot, patches, grid, log_total)


def per_device(
    chars,
    lengths,
    char_table,
    conv_weight,
    conv_bias,
    highway_weight,
    highway_bias,
    proj_weight,
    proj_bias,
    position,
    norm_gain,
    norm_bias,
    query_key_value_weight,
    attention_output_weight,
    feedforward_input_weight,
    feedforward_input_bias,
    feedforward_output_weight,
    cotangent,
):
    gathered = (
        lax.all_gather(highway_weight, "dp", axis=1, tiled=True),
        lax.all_gather(highway_bias, "dp", axis=1, tiled=True),
        lax.all_gather(proj_weight, "dp", axis=0, tiled=True),
        lax.all_gather(proj_bias, "dp", axis=0, tiled=True),
        lax.all_gather(query_key_value_weight, "dp", axis=0, tiled=True),
        lax.all_gather(attention_output_weight, "dp", axis=0, tiled=True),
        lax.all_gather(feedforward_input_weight, "dp", axis=0, tiled=True),
        lax.all_gather(feedforward_input_bias, "dp", axis=0, tiled=True),
        lax.all_gather(feedforward_output_weight, "dp", axis=0, tiled=True),
        lax.all_gather(norm_gain, "dp", axis=1, tiled=True),
        lax.all_gather(norm_bias, "dp", axis=1, tiled=True),
    )
    (
        highway_full,
        highway_bias_full,
        proj_full,
        proj_bias_full,
        qkv_full,
        out_full,
        inner_full,
        inner_bias_full,
        outer_full,
        gain_full,
        shift_full,
    ) = gathered
    gain_full = gain_full.astype(jnp.float32)
    shift_full = shift_full.astype(jnp.float32)
    seqs, quarter, dmodel = cotangent.shape
    full_len = chars.shape[1]
    letters = chars.shape[2]
    tokens = seqs * quarter
    filt_index = lax.axis_index("filt")
    offset = filt_index * conv_weight.shape[1]
    word_ids = chars.reshape(seqs * full_len, letters)
    channels = offset + jnp.arange(conv_weight.shape[1], dtype=jnp.int32)
    widths = channel_widths(channels)
    tap_index = jnp.arange(conv_weight.shape[0], dtype=jnp.int32) // char_table.shape[1]
    tap_keep = tap_index[:, None] < widths[None, :]
    masked_weight = jnp.where(tap_keep, conv_weight, 0)
    valid = jnp.arange(letters, dtype=jnp.int32)[:, None] <= letters - widths[None, :]
    counts = (letters - widths + 1).astype(jnp.float32)
    bias_row = conv_bias.astype(jnp.float32)
    word_count = word_ids.shape[0]
    block_rows = math.gcd(word_count, 128)
    block_count = word_count // block_rows
    id_blocks = word_ids.reshape(block_count, block_rows, letters)

    def forward_block(carried, block_ids):
        onehot, patches, grid, log_total = char_grid(
            block_ids, char_table, masked_weight, bias_row, valid
        )
        return (
            carried,
            exact_gaussian_activation(log_total - jnp.log(counts)).astype(jnp.bfloat16),
        )

    unused, acts = lax.scan(forward_block, jnp.zeros((), jnp.float32), id_blocks)
    features = lax.all_to_all(
        acts.reshape(seqs, full_len, -1), "filt", split_axis=1, concat_axis=2, tiled=True
    )
    features = features.reshape(tokens, -1)
    hidden = features.astype(jnp.float32)
    layer = 0
    gates = jnp.dot(
        hidden.astype(jnp.bfloat16), highway_full[layer], preferred_element_type=jnp.float32
    ) + highway_bias_full[layer].astype(jnp.float32)
    kept_layers = [(hidden, gates)]
    hidden = highway_mix(hidden, gates)
    hidden_low = hidden.astype(jnp.bfloat16)
    projected = jnp.dot(
        hidden_low, proj_full, preferred_element_type=jnp.float32
    ) + proj_bias_full.astype(jnp.float32)
    summed = (projected.reshape(seqs, quarter, dmodel) + position.astype(jnp.float32)).reshape(
        tokens, dmodel
    )
    first_operand, norm_zero_pull = jax.vjp(layer_norm, summed, gain_full[0], shift_full[0])
    first_low = first_operand.astype(jnp.bfloat16)
    packed_projection = jnp.dot(first_low, qkv_full, preferred_element_type=jnp.float32).astype(
        jnp.bfloat16
    )
    heads = dmodel // HD
    queries = packed_projection[:, :dmodel].reshape(seqs, quarter, heads, HD)
    keys_local = packed_projection[:, dmodel : 2 * dmodel].reshape(seqs, quarter, dmodel)
    values_local = packed_projection[:, 2 * dmodel :].reshape(seqs, quarter, dmodel)
    keys_all, values_all = (
        lax.all_gather(keys_local, "filt", axis=1, tiled=True),
        lax.all_gather(values_local, "filt", axis=1, tiled=True),
    )
    keys_all = keys_all.reshape(seqs, full_len, heads, HD)
    values_all = values_all.reshape(seqs, full_len, heads, HD)
    key_ok = jnp.arange(full_len, dtype=jnp.int32)[None, :] < lengths[:, None]
    scale = HD ** (-0.5)

    def attention_probs():
        scores = (
            jnp.einsum("sqhd,skhd->shqk", queries, keys_all, preferred_element_type=jnp.float32)
            * scale
        )
        scores = jnp.where(key_ok[:, None, None, :], scores, -1e30)
        row_top = jnp.max(scores, axis=-1, keepdims=True)
        log_total = row_top + jnp.log(jnp.sum(jnp.exp(scores - row_top), axis=-1, keepdims=True))
        return jnp.exp(scores - log_total)

    probs = attention_probs()
    probs_low = probs.astype(jnp.bfloat16)
    attention_result = (
        jnp.einsum("shqk,skhd->sqhd", probs_low, values_all, preferred_element_type=jnp.float32)
        .astype(jnp.bfloat16)
        .reshape(tokens, dmodel)
    )
    mixed_hidden = jnp.dot(attention_result, out_full, preferred_element_type=jnp.float32)
    second_operand, norm_one_pull = jax.vjp(
        layer_norm, first_operand + mixed_hidden, gain_full[1], shift_full[1]
    )
    second_low = second_operand.astype(jnp.bfloat16)
    inner_activation = jnp.dot(
        second_low, inner_full, preferred_element_type=jnp.float32
    ) + inner_bias_full.astype(jnp.float32)
    active = exact_gaussian_activation(inner_activation).astype(jnp.bfloat16)
    outer_projection = jnp.dot(active, outer_full, preferred_element_type=jnp.float32)
    top_out, norm_two_pull = jax.vjp(
        layer_norm, second_operand + outer_projection, gain_full[2], shift_full[2]
    )
    encoded = top_out.astype(jnp.bfloat16).reshape(seqs, quarter, dmodel)
    upstream = cotangent.reshape(tokens, dmodel).astype(jnp.float32)
    d_res_two, d_gain_two, d_shift_two = norm_two_pull(upstream)
    d_outer = d_res_two.astype(jnp.bfloat16)
    grad_outer_w = jnp.einsum("nf,nd->fd", active, d_outer, preferred_element_type=jnp.float32)
    d_active = jnp.einsum("nd,fd->nf", d_outer, outer_full, preferred_element_type=jnp.float32)
    d_inner = gelu_back(inner_activation, d_active).astype(jnp.bfloat16)
    grad_inner_w = jnp.einsum("nd,nf->df", second_low, d_inner, preferred_element_type=jnp.float32)
    grad_inner_b = jnp.sum(d_inner.astype(jnp.float32), axis=0)
    d_second = d_res_two + jnp.einsum(
        "nf,df->nd", d_inner, inner_full, preferred_element_type=jnp.float32
    )
    d_res_one, d_gain_one, d_shift_one = norm_one_pull(d_second)
    d_mixed = d_res_one.astype(jnp.bfloat16)
    grad_out_w = jnp.einsum(
        "nd,ne->de", attention_result, d_mixed, preferred_element_type=jnp.float32
    )
    d_attended = jnp.einsum("ne,de->nd", d_mixed, out_full, preferred_element_type=jnp.float32)
    d_attended = d_attended.astype(jnp.bfloat16).reshape(seqs, quarter, heads, HD)
    probs = attention_probs()
    probs_low = probs.astype(jnp.bfloat16)
    d_values = jnp.einsum(
        "shqk,sqhd->skhd", probs_low, d_attended, preferred_element_type=jnp.float32
    )
    d_probs = jnp.einsum(
        "sqhd,skhd->shqk", d_attended, values_all, preferred_element_type=jnp.float32
    )
    row_inner = jnp.sum(d_probs * probs, axis=-1, keepdims=True)
    d_scores = (probs * (d_probs - row_inner)).astype(jnp.bfloat16)
    d_queries = (
        jnp.einsum("shqk,skhd->sqhd", d_scores, keys_all, preferred_element_type=jnp.float32)
        * scale
    )
    d_keys = (
        jnp.einsum("shqk,sqhd->skhd", d_scores, queries, preferred_element_type=jnp.float32) * scale
    )
    d_keys, d_values = (
        lax.psum_scatter(
            d_keys.reshape(seqs, full_len, dmodel).astype(jnp.bfloat16),
            "filt",
            scatter_dimension=1,
            tiled=True,
        ).astype(jnp.float32),
        lax.psum_scatter(
            d_values.reshape(seqs, full_len, dmodel).astype(jnp.bfloat16),
            "filt",
            scatter_dimension=1,
            tiled=True,
        ).astype(jnp.float32),
    )
    d_packed = jnp.concatenate(
        [
            d_queries.reshape(tokens, dmodel),
            d_keys.reshape(tokens, dmodel),
            d_values.reshape(tokens, dmodel),
        ],
        axis=1,
    ).astype(jnp.bfloat16)
    grad_qkv_w = jnp.einsum("nd,ne->de", first_low, d_packed, preferred_element_type=jnp.float32)
    d_first = d_res_one + jnp.einsum(
        "ne,de->nd", d_packed, qkv_full, preferred_element_type=jnp.float32
    )
    d_summed, d_gain_zero, d_shift_zero = norm_zero_pull(d_first)
    grad_pos = jnp.sum(d_summed.reshape(seqs, quarter, dmodel), axis=0)
    d_projected = d_summed.astype(jnp.bfloat16)
    grad_proj_w = jnp.einsum(
        "nf,nd->fd", hidden_low, d_projected, preferred_element_type=jnp.float32
    )
    grad_proj_b = jnp.sum(d_projected.astype(jnp.float32), axis=0)
    d_hidden = jnp.einsum("nd,fd->nf", d_projected, proj_full, preferred_element_type=jnp.float32)
    highway_grads = []
    highway_bias_grads = []
    for layer in reversed(range(highway_full.shape[0])):
        layer_in, gates = kept_layers[layer]
        d_in, d_gates = jax.vjp(highway_mix, layer_in, gates)[1](d_hidden)
        d_gates = d_gates.astype(jnp.bfloat16)
        highway_grads.insert(
            0,
            jnp.einsum(
                "nf,ng->fg",
                layer_in.astype(jnp.bfloat16),
                d_gates,
                preferred_element_type=jnp.float32,
            ),
        )
        highway_bias_grads.insert(0, jnp.sum(d_gates.astype(jnp.float32), axis=0))
        d_hidden = d_in + jnp.einsum(
            "ng,fg->nf", d_gates, highway_full[layer], preferred_element_type=jnp.float32
        )
    d_features = d_hidden.astype(jnp.bfloat16)
    d_acts = lax.all_to_all(
        d_features.reshape(seqs, quarter, -1), "filt", split_axis=2, concat_axis=1, tiled=True
    )
    d_blocks = d_acts.reshape(block_count, block_rows, -1)
    depth = char_table.shape[1]

    def backward_block(totals, item):
        block_ids, block_grad = item
        onehot, patches, grid, log_total = char_grid(
            block_ids, char_table, masked_weight, bias_row, valid
        )
        d_pooled = gelu_back(log_total - jnp.log(counts), block_grad.astype(jnp.float32))
        position_weights = jnp.exp(grid - log_total[:, None, :])
        d_grid = (position_weights * d_pooled[:, None, :]).astype(jnp.bfloat16)
        grad_weight = totals[0] + jnp.einsum(
            "wpk,wpc->kc", patches, d_grid, preferred_element_type=jnp.float32
        )
        grad_bias = totals[1] + jnp.sum(d_grid.astype(jnp.float32), axis=(0, 1))
        d_patch = jnp.einsum(
            "wpc,kc->wpk", d_grid, masked_weight, preferred_element_type=jnp.float32
        )
        pieces = [
            jnp.pad(
                d_patch[:, :, shift_tap * depth : (shift_tap + 1) * depth],
                ((0, 0), (shift_tap, KW - 1 - shift_tap), (0, 0)),
            )
            for shift_tap in range(KW)
        ]
        d_embedded = reduce(jnp.add, pieces)[:, :letters, :]
        grad_table = totals[2] + jnp.einsum(
            "wpv,wpd->vd", onehot.astype(jnp.float32), d_embedded, precision=lax.Precision.HIGHEST
        )
        return ((grad_weight, grad_bias, grad_table), None)

    start = (
        jnp.zeros(masked_weight.shape, jnp.float32),
        jnp.zeros(bias_row.shape, jnp.float32),
        jnp.zeros(char_table.shape, jnp.float32),
    )
    char_totals, unused_rows = lax.scan(backward_block, start, (id_blocks, d_blocks))
    conv_grad_w = jnp.where(tap_keep, char_totals[0], 0.0)
    conv_grad_b = char_totals[1]
    conv_grad_w, conv_grad_b, grad_pos, table_grad = lax.psum(
        (conv_grad_w, conv_grad_b, grad_pos, char_totals[2]), "dp"
    )
    highway_stack = jnp.stack(highway_grads)
    highway_bias_stack = jnp.stack(highway_bias_grads)
    gain_stack = jnp.stack([d_gain_zero, d_gain_one, d_gain_two])
    shift_stack = jnp.stack([d_shift_zero, d_shift_one, d_shift_two])
    shards = (
        lax.psum_scatter(highway_stack, "dp", scatter_dimension=1, tiled=True),
        lax.psum_scatter(highway_bias_stack, "dp", scatter_dimension=1, tiled=True),
        lax.psum_scatter(grad_proj_w, "dp", scatter_dimension=0, tiled=True),
        lax.psum_scatter(grad_proj_b, "dp", scatter_dimension=0, tiled=True),
        lax.psum_scatter(grad_qkv_w, "dp", scatter_dimension=0, tiled=True),
        lax.psum_scatter(grad_out_w, "dp", scatter_dimension=0, tiled=True),
        lax.psum_scatter(grad_inner_w, "dp", scatter_dimension=0, tiled=True),
        lax.psum_scatter(grad_inner_b, "dp", scatter_dimension=0, tiled=True),
        lax.psum_scatter(grad_outer_w, "dp", scatter_dimension=0, tiled=True),
        lax.psum_scatter(gain_stack, "dp", scatter_dimension=1, tiled=True),
        lax.psum_scatter(shift_stack, "dp", scatter_dimension=1, tiled=True),
    )
    summed_all = (
        lax.psum(shards[0].astype(jnp.bfloat16), "filt").astype(jnp.float32),
        lax.psum(shards[1].astype(jnp.bfloat16), "filt").astype(jnp.float32),
        lax.psum(shards[2].astype(jnp.bfloat16), "filt").astype(jnp.float32),
        lax.psum(shards[3].astype(jnp.bfloat16), "filt").astype(jnp.float32),
        lax.psum(shards[4].astype(jnp.bfloat16), "filt").astype(jnp.float32),
        lax.psum(shards[5].astype(jnp.bfloat16), "filt").astype(jnp.float32),
        lax.psum(shards[6].astype(jnp.bfloat16), "filt").astype(jnp.float32),
        lax.psum(shards[7].astype(jnp.bfloat16), "filt").astype(jnp.float32),
        lax.psum(shards[8].astype(jnp.bfloat16), "filt").astype(jnp.float32),
        lax.psum(shards[9].astype(jnp.bfloat16), "filt").astype(jnp.float32),
        lax.psum(shards[10].astype(jnp.bfloat16), "filt").astype(jnp.float32),
        lax.psum(table_grad.astype(jnp.bfloat16), "filt").astype(jnp.float32),
    )
    (
        g_highway,
        g_highway_b,
        g_proj,
        g_proj_b,
        g_qkv,
        g_out,
        g_inner,
        g_inner_b,
        g_outer,
        g_gain,
        g_shift,
        g_table,
    ) = summed_all
    return (
        encoded,
        g_table,
        conv_grad_w,
        conv_grad_b,
        g_highway,
        g_highway_b,
        g_proj,
        g_proj_b,
        grad_pos,
        g_gain,
        g_shift,
        g_qkv,
        g_out,
        g_inner,
        g_inner_b,
        g_outer,
    )


def solution(mesh):
    return jax.shard_map(
        per_device,
        mesh=mesh,
        in_specs=(
            P("dp", None, None),
            P("dp"),
            P(),
            P(None, "filt"),
            P("filt"),
            P(None, "dp", None),
            P(None, "dp"),
            P("dp", None),
            P("dp"),
            P("filt", None),
            P(None, "dp"),
            P(None, "dp"),
            P("dp", None),
            P("dp", None),
            P("dp", None),
            P("dp"),
            P("dp", None),
            P("dp", "filt", None),
        ),
        out_specs=(
            P("dp", "filt", None),
            P(),
            P(None, "filt"),
            P("filt"),
            P(None, "dp", None),
            P(None, "dp"),
            P("dp", None),
            P("dp"),
            P("filt", None),
            P(None, "dp"),
            P(None, "dp"),
            P("dp", None),
            P("dp", None),
            P("dp", None),
            P("dp"),
            P("dp", None),
        ),
        check_vma=False,
    )
```

profile of v0, /device:TPU:0, one launch (start us, length us, event | category | flops | bytes accessed | tf_op | source)
XLA Modules:
  0.0 2225.6 jit_solution(4336627798386934143)
XLA Ops:
  11.9 28.6 %while.30 = (s32[]{:T(128)}, bf16[4,128,512]{2,1,0:T(8,128)(2,1)S(1)}, s32[4,128,50]{1,2,0:T(8,128)S(1)}, bf16[262,16]{0,1:T(8,128)(2,1)S(1)}, bf16[112,512]{1,0...) while((s32[]{:T(128)}, bf16[4,128,512]{2,1,0:T(8,128)(2,1)S(1)}, ...), condition=%wide.region_3.4_spmd.clone, body=%wide.region_0.3_spmd.clone.sunk | while | flops 816673792 | bytes 32244016 | solution.py:142
  51.3 29.1 %all-gather.4 = bf16[8,1,384]{2,1,0:T(2,128)(2,1)S(1)} all-gather(bf16[1,1,384]{2,1,0:T(2,128)(2,1)S(1)} %reshape.805), channel_id=1, replica_groups=mesh['dp'=8,'filt'=4] {'dp'}, dimensions={0}, use_global_device_ids=true | all-gather | bytes 6912 | tf_op jit(solution)/shard_map/all_gather | solution.py:93
  81.9 18.5 all-reduce.11
  100.4 26.5 %all_gather.40 = bf16[1,4096]{1,0:T(2,128)(2,1)S(1)} all-gather(bf16[1,512]{1,0:T(2,128)(2,1)S(1)} %copy-done.46), channel_id=1, replica_groups=mesh['dp'=8,'filt'=4] {'dp'}, dimensions={1}, use_global_device_ids=true | all-gather | bytes 9216 | tf_op jit(solution)/shard_map/all_gather | solution.py:87
  126.9 17.5 all-gather.3
  144.5 17.6 all-gather.2
  164.1 77.4 %all-gather.12.cloned.1.call-done = bf16[1,2048,4096]{2,1,0:T(8,128)(2,1)} async-done(((bf16[1,256,4096]{2,1,0:T(8,128)(2,1)}), bf16[1,2048,4096]{2,1,0:T(8,128)(2,1)}) %all-gather.12.cloned.1.call-update) | async-done | bytes 16777232 | tf_op jit(solution)/shard_map/all_gather | solution.py:86
  254.3 48.0 %all-gather.14.cloned.1.call-done = bf16[2048,768]{1,0:T(8,128)(2,1)} async-done(((bf16[256,768]{1,0:T(8,128)(2,1)}), bf16[2048,768]{1,0:T(8,128)(2,1)}) %all-gather.14.cloned.1.call-update) | async-done | bytes 3145744 | tf_op jit(solution)/shard_map/all_gather | solution.py:88
  305.1 63.2 %all-gather.16.cloned.1.call-done = bf16[768,2304]{1,0:T(8,128)(2,1)} async-done(((bf16[96,2304]{1,0:T(8,128)(2,1)}), bf16[768,2304]{1,0:T(8,128)(2,1)}) %all-gather.16.cloned.1.call-update) | async-done | bytes 3538960 | tf_op jit(solution)/shard_map/all_gather | solution.py:90
  395.9 14.0 all-gather.18.cloned.1.call-done
  412.8 77.9 %all-gather.20.cloned.1.call-done = bf16[768,3072]{1,0:T(8,128)(2,1)} async-done(((bf16[96,3072]{1,0:T(8,128)(2,1)}), bf16[768,3072]{1,0:T(8,128)(2,1)}) %all-gather.20.cloned.1.call-update) | async-done | bytes 4718608 | tf_op jit(solution)/shard_map/all_gather | solution.py:92
  499.2 71.6 %all-gather.22.cloned.1.call-done = bf16[3072,768]{1,0:T(8,128)(2,1)} async-done(((bf16[384,768]{1,0:T(8,128)(2,1)}), bf16[3072,768]{1,0:T(8,128)(2,1)}) %all-gather.22.cloned.1.call-update) | async-done | bytes 4718608 | tf_op jit(solution)/shard_map/all_gather | solution.py:94
  606.9 9.5 reduce-scatter.36.cloned.1.call-done
  618.0 25.0 %reduce-scatter.34.cloned.1.call-done = bf16[128,768]{1,0:T(8,128)(2,1)} async-done(((bf16[512,768]{1,0:T(8,128)(2,1)}), bf16[128,768]{1,0:T(8,128)(2,1)}) %reduce-scatter.34.cloned.1.call-update) | async-done | bytes 196624
  677.4 13.7 convolution_bitcast_fusion.1
  691.2 12.3 fusion.86
  704.3 11.6 reduce.22
  733.1 103.5 %reduce-scatter.24.cloned.1.call-done = f32[256,768]{1,0:T(8,128)} async-done(((f32[2048,768]{1,0:T(8,128)}), f32[256,768]{1,0:T(8,128)}) %reduce-scatter.24.cloned.1.call-update) | async-done | bytes 786448 | tf_op jit(solution)/shard_map/reduce_scatter | solution.py:351
  838.5 130.0 %reduce-scatter.26.cloned.1.call-done = f32[96,2304]{1,0:T(8,128)} async-done(((f32[768,2304]{1,0:T(8,128)}), f32[96,2304]{1,0:T(8,128)}) %reduce-scatter.26.cloned.1.call-update) | async-done | bytes 884752 | tf_op jit(solution)/shard_map/reduce_scatter | solution.py:353
  970.4 164.3 %reduce-scatter.30.cloned.1.call-done = f32[96,3072]{1,0:T(8,128)} async-done(((f32[768,3072]{1,0:T(8,128)}), f32[96,3072]{1,0:T(8,128)}) %reduce-scatter.30.cloned.1.call-update) | async-done | bytes 1179664 | tf_op jit(solution)/shard_map/reduce_scatter | solution.py:355
  1136.9 164.3 %reduce-scatter.32.cloned.1.call-done = f32[384,768]{1,0:T(8,128)} async-done(((f32[3072,768]{1,0:T(8,128)}), f32[384,768]{1,0:T(8,128)}) %reduce-scatter.32.cloned.1.call-update) | async-done | bytes 1179664 | tf_op jit(solution)/shard_map/reduce_scatter | solution.py:357
  1303.3 544.4 %reduce-scatter.22.cloned.1.call-done = f32[1,256,4096]{2,1,0:T(8,128)} async-done(((f32[1,2048,4096]{2,1,0:T(8,128)}), f32[1,256,4096]{2,1,0:T(8,128)}) %reduce-scatter.22.cloned.1.call-update) | async-done | bytes 4194320 | tf_op jit(solution)/shard_map/reduce_scatter | solution.py:349
  1852.2 125.3 %while.31 = (s32[]{:T(128)}, f32[112,512]{1,0:T(8,128)S(1)}, f32[512]{0:T(512)S(1)}, f32[262,16]{0,1:T(8,128)S(1)}, s32[4,128,50]{1,2,0:T(8,128)}, /*index=5*/bf...) while((s32[]{:T(128)}, f32[112,512]{1,0:T(8,128)S(1)}, ...), condition=%wide.region_25.26_spmd.clone, body=%wide.region_21.25_spmd.clone.sunk | while | flops 2619329792 | bytes 157400272 | solution.py:338
  1862.4 10.3 convert_reduce_fusion.6
  1893.8 10.3 convert_reduce_fusion.6
  1925.0 10.3 convert_reduce_fusion.6
  1956.3 10.3 convert_reduce_fusion.6
  1981.5 65.3 %reduce-scatter.38.cloned.1.call-done = f32[512,1]{1,0:T(8,128)} async-done(((f32[4096,1]{1,0:T(8,128)}), f32[512,1]{1,0:T(8,128)}) %reduce-scatter.38.cloned.1.call-update) | async-done | bytes 2064
  2047.9 35.9 %all-reduce.14 = (bf16[262,16]{0,1:T(8,128)(2,1)S(1)}, f32[512]{0:T(512)}, bf16[768]{0:T(1024)(128)(2,1)S(1)}, bf16[3072]{0:T(1024)(128)(2,1)S(1)}) all-reduce(f32[262,16]{0,1:T(8,128)S(1)} %get-tuple-element.262, f32[512]{0:T(512)S(1)} %get-tuple-element.264, f32[768]{0:T(1024)S(1)} %copy-done.44, ...), channel_id=1, replica_groups=mesh['dp'=8,'filt'=4] {'dp'}, use_global_device_ids=true, to_apply=%region_26.27 | all-reduce | flops 8544 | bytes 52288 | tf_op jit(solution)/shard_map/psum | solution.py:341
  2083.9 11.4 all-reduce.16
  2098.7 39.1 %all-reduce.23.cloned.1.call-done = (bf16[1,256,4096]{2,1,0:T(8,128)(2,1)}, bf16[256,768]{1,0:T(8,128)(2,1)}, bf16[96,2304]{1,0:T(8,128)(2,1)}, bf16[96,768]{1,0...) async-done(((bf16[1,256,4096]{2,1,0:T(8,128)(2,1)}, bf16[256,768]{1,0:T(8,128)(2,1)}, bf16[96,2304]{1,0:T(8,128)(2,1)}, bf16[96,768]{1,0:T(8,128)(2,1)}, ...) | async-done | bytes 4259856 | tf_op jit(solution)/shard_map/psum | solution.py:362
  2146.8 68.7 %all-reduce.21.cloned.1.call-done = (f32[112,512]{1,0:T(8,128)}, f32[128,768]{1,0:T(8,128)}) async-done(((f32[112,512]{1,0:T(8,128)}, f32[128,768]{1,0:T(8,128)}), (f32[112,512]{1,0:T(8,128)}, f32[128,768]{1,0:T(8,128)})) %all-reduce.21.cloned.1.call-update) | async-done | bytes 622608 | tf_op jit(solution)/shard_map/psum | solution.py:341
  (468 shorter events, 305.3 us)
Async XLA Ops:
  7.2 234.3 %all-gather.12.cloned.1.call-start = ((), (), s32[]{:S(2)}) async-start(), calls=%async_computation.13 | async-start | bytes 18874368 | tf_op jit(solution)/shard_map/all_gather | solution.py:86
  8.0 294.4 %all-gather.14.cloned.1.call-start = ((), (), s32[]{:S(2)}) async-start(), calls=%async_computation.14 | async-start | bytes 3538944 | tf_op jit(solution)/shard_map/all_gather | solution.py:88
  8.7 359.6 %all-gather.16.cloned.1.call-start = ((), (), s32[]{:S(2)}) async-start(), calls=%async_computation.15 | async-start | bytes 3981312 | tf_op jit(solution)/shard_map/all_gather | solution.py:90
  9.4 400.5 %all-gather.18.cloned.1.call-start = ((), (), s32[]{:S(2)}) async-start(), calls=%async_computation.16 | async-start | bytes 1327104 | tf_op jit(solution)/shard_map/all_gather | solution.py:91
  10.0 480.7 %all-gather.20.cloned.1.call-start = ((), (), s32[]{:S(2)}) async-start(), calls=%async_computation.17 | async-start | bytes 5308416 | tf_op jit(solution)/shard_map/all_gather | solution.py:92
  10.6 560.2 %all-gather.22.cloned.1.call-start = ((), (), s32[]{:S(2)}) async-start(), calls=%async_computation.18 | async-start | bytes 5308416 | tf_op jit(solution)/shard_map/all_gather | solution.py:94
  41.8 58.6 %copy-start.46 = (bf16[1,512]{1,0:T(2,128)(2,1)S(1)}, bf16[1,512]{1,0:T(2,128)(2,1)}, u32[]{:S(2)}) copy-start(bf16[1,512]{1,0:T(2,128)(2,1)} %param.28) | copy-start | bytes 3076
  41.8 85.1 %copy-start.51 = (bf16[3,96]{1,0:T(4,128)(2,1)S(1)}, bf16[3,96]{1,0:T(4,128)(2,1)}, u32[]{:S(2)}) copy-start(bf16[3,96]{1,0:T(4,128)(2,1)} %param.33) | copy-start | bytes 1732
  41.8 102.7 %copy-start.52 = (bf16[3,96]{1,0:T(4,128)(2,1)S(1)}, bf16[3,96]{1,0:T(4,128)(2,1)}, u32[]{:S(2)}) copy-start(bf16[3,96]{1,0:T(4,128)(2,1)} %param.32) | copy-start | bytes 1732
  46.9 116.0 %all-to-all-start = ((bf16[4,2,32768]{2,1,0:T(2,128)(2,1)}), bf16[4,2,32768]{2,1,0:T(2,128)(2,1)S(1)}, u32[]{:S(2)}, u32[]{:S(2)}) async-start(bf16[4,2,32768]{2,1,0:T(2,128)(2,1)} %reshape.839), calls=%async_computation | async-start | bytes 1048576 | tf_op jit(solution)/shard_map/all_to_all | solution.py:143
  51.1 565.3 %reduce-scatter.36.cloned.1.call-start = ((), (), s32[]{:S(2)}) async-start(), calls=%async_computation.26 | async-start | bytes 983040
  164.1 85.6 %copy-start.9 = (bf16[16,8,4,512]{3,1,2,0:T(8,128)(2,1)}, bf16[16,8,4,512]{3,1,2,0:T(8,128)(2,1)S(1)}, u32[]{:S(2)}) copy-start(bf16[16,8,4,512]{3,1,2,0:T(8,128)(2,1)S(1)} %copy.109) | copy-start | bytes 1572868
  251.0 51.3 %copy-start.38 = (bf16[128,768]{1,0:T(8,128)(2,1)S(1)}, bf16[128,768]{1,0:T(8,128)(2,1)}, u32[]{:S(2)}) copy-start(bf16[128,768]{1,0:T(8,128)(2,1)} %param.31) | copy-start | bytes 589828
  254.3 50.6 %copy-start.13 = (bf16[128,2048]{1,0:T(8,128)(2,1)}, bf16[128,2048]{1,0:T(8,128)(2,1)S(1)}, u32[]{:S(2)}) copy-start(bf16[128,2048]{1,0:T(8,128)(2,1)S(1)} %get-tuple-element.488) | copy-start | bytes 1572868
  304.9 66.1 %copy-start.2 = (f32[128,768]{1,0:T(8,128)}, f32[128,768]{1,0:T(8,128)S(1)}, u32[]{:S(2)}) copy-start(f32[128,768]{1,0:T(8,128)S(1)} %get-tuple-element.518) | copy-start | bytes 1179652
  594.9 48.1 %reduce-scatter.34.cloned.1.call-start = ((), (), s32[]{:S(2)}) async-start(), calls=%async_computation.25 | async-start | bytes 983040
  602.5 128.9 %reduce-scatter.28.cloned.1.call-start = ((), (), s32[]{:S(2)}) async-start(), calls=%async_computation.22 | async-start | bytes 2654208 | tf_op jit(solution)/shard_map/reduce_scatter | solution.py:354
  604.7 231.9 %reduce-scatter.24.cloned.1.call-start = ((), (), s32[]{:S(2)}) async-start(), calls=%async_computation.20 | async-start | bytes 7077888 | tf_op jit(solution)/shard_map/reduce_scatter | solution.py:351
  652.8 315.6 %reduce-scatter.26.cloned.1.call-start = ((), (), s32[]{:S(2)}) async-start(), calls=%async_computation.21 | async-start | bytes 7962624 | tf_op jit(solution)/shard_map/reduce_scatter | solution.py:353
  657.1 477.6 %reduce-scatter.30.cloned.1.call-start = ((), (), s32[]{:S(2)}) async-start(), calls=%async_computation.23 | async-start | bytes 10616832 | tf_op jit(solution)/shard_map/reduce_scatter | solution.py:355
  663.4 637.7 %reduce-scatter.32.cloned.1.call-start = ((), (), s32[]{:S(2)}) async-start(), calls=%async_computation.24 | async-start | bytes 10616832 | tf_op jit(solution)/shard_map/reduce_scatter | solution.py:357
  669.7 1178.0 %reduce-scatter.22.cloned.1.call-start = ((), (), s32[]{:S(2)}) async-start(), calls=%async_computation.19 | async-start | bytes 37748736 | tf_op jit(solution)/shard_map/reduce_scatter | solution.py:349
  716.8 12.4 all-to-all-start.1
  720.4 1259.3 %reduce-scatter.40.cloned.1.call-start = ((), (), s32[]{:S(2)}) async-start(), calls=%async_computation.28 | async-start | bytes 442368
  721.5 1259.0 %reduce-scatter.42.cloned.1.call-start = ((), (), s32[]{:S(2)}) async-start(), calls=%async_computation.29 | async-start | bytes 442368
  722.6 1324.2 %reduce-scatter.38.cloned.1.call-start = ((), (), s32[]{:S(2)}) async-start(), calls=%async_computation.27 | async-start | bytes 2359296
  724.8 1413.0 %all-reduce.23.cloned.1.call-start = ((), (), s32[]{:S(2)}) async-start(), calls=%async_computation.31 | async-start | bytes 8519680 | tf_op jit(solution)/shard_map/psum | solution.py:362
  1851.5 364.0 %all-reduce.21.cloned.1.call-start = ((), (), s32[]{:S(2)}) async-start(), calls=%async_computation.30 | async-start | bytes 1245184 | tf_op jit(solution)/shard_map/psum | solution.py:341
  1852.2 125.4 %copy-start.43 = (s32[512]{0:T(512)S(1)}, s32[512]{0:T(512)}, u32[]{:S(2)}) copy-start(s32[512]{0:T(512)} %copy-done.42) | copy-start | bytes 6148
  1852.2 125.4 %copy-start.49 = (s32[112]{0:T(128)S(1)}, s32[112]{0:T(128)}, u32[]{:S(2)}) copy-start(s32[112]{0:T(128)} %copy-done.48) | copy-start | bytes 1348
  1852.2 195.7 %copy-start.44 = (f32[768]{0:T(1024)S(1)}, f32[768]{0:T(1024)}, u32[]{:S(2)}) copy-start(f32[768]{0:T(1024)} %get-tuple-element.478) | copy-start | bytes 9220
  1852.2 195.7 %copy-start.45 = (f32[3072]{0:T(1024)S(1)}, f32[3072]{0:T(1024)}, u32[]{:S(2)}) copy-start(f32[3072]{0:T(1024)} %get-tuple-element.531) | copy-start | bytes 36868
  (66 other events, 336.8 us)
Sparse Core Ops, SparseCore 0:
  10.1 231.3 all-gather.11
  243.7 58.5 all-gather.13
  304.5 63.7 all-gather.15
  370.4 39.5 all-gather.17
  412.0 78.6 all-gather.19
  492.7 78.0 all-gather.21
  595.0 21.3 reduce-scatter.35
  619.7 23.2 reduce-scatter.33
  647.1 69.0 reduce-scatter.27
  719.5 116.9 reduce-scatter.23
  840.3 128.1 reduce-scatter.25
  972.3 162.3 reduce-scatter.29
  1138.7 162.3 reduce-scatter.31
  1305.3 542.4 reduce-scatter.21
  1851.8 60.5 reduce-scatter.39
  1915.8 60.4 reduce-scatter.41
  1980.0 66.7 reduce-scatter.37
  2050.8 86.9 all-reduce.22
  2141.9 73.6 all-reduce.20
where the time goes:
time: 2240 us; the launch traced here: 2230 us
  waiting for transfers between devices  1670 us (75%)
  blocking collectives  174 us (8%)
  matrix products  163 us (7%)
  other arithmetic  117 us (5%)
  local copies, waits for them, and re-layouts  68.9 us (3%)
    reduce_scatter x1, waiting for transfers between devices, per_device(): lax.psum_scatter(highway_stack, 'dp', scatter_dimension=1, tiled=True)  544 us
    reduce_scatter x1, waiting for transfers between devices, per_device(): lax.psum_scatter(grad_outer_w, 'dp', scatter_dimension=0, tiled=True)  164 us
    reduce_scatter x1, waiting for transfers between devices, per_device(): lax.psum_scatter(grad_inner_w, 'dp', scatter_dimension=0, tiled=True)  164 us
    reduce_scatter x1, waiting for transfers between devices, per_device(): lax.psum_scatter(grad_qkv_w, 'dp', scatter_dimension=0, tiled=True)  130 us
    unnamed x24, waiting for transfers between devices  104 us
    reduce_scatter x1, waiting for transfers between devices, per_device(): lax.psum_scatter(grad_proj_w, 'dp', scatter_dimension=0, tiled=True)  104 us
    all_gather x1, waiting for transfers between devices, per_device(): lax.all_gather(feedforward_input_weight, 'dp', axis=0, tiled=True)  77.9 us
    all_gather x1, waiting for transfers between devices, per_device(): lax.all_gather(highway_weight, 'dp', axis=1, tiled=True)  77.4 us
  transfers between devices with their start and end apart: 21, of which 17 were waited for; matrix products, arithmetic and copies ran while one was open for 13% of the time, Pallas kernels for 0%

commit v1 on v0

v1 whole, which is shorter than its diff:
```python
from functools import reduce
import math

import jax
import jax.numpy as jnp
from jax import lax
from jax.sharding import PartitionSpec as P

KW = 7
NF = 2048
HD = 64


eps_norm = 1e-12


def exact_gaussian_activation(values):
    return jax.nn.gelu(values, approximate=False)


def gelu_back(values, upstream):
    return jax.vjp(exact_gaussian_activation, values)[1](upstream)[0]


def layer_norm(values, scale, offset):
    center = values - jnp.mean(values, axis=-1, keepdims=True)
    spread = jnp.mean(center * center, axis=-1, keepdims=True)
    return center * lax.rsqrt(spread + eps_norm) * scale + offset


def channel_widths(channels):
    widths = jnp.ones_like(channels)
    for power in range(6):
        widths = widths + (channels >= NF * 2**power // 64).astype(jnp.int32)
    return widths


def highway_mix(hidden, gates):
    width = hidden.shape[1]
    carry_gate = jax.nn.sigmoid(gates[:, width:])
    return carry_gate * hidden + (1.0 - carry_gate) * exact_gaussian_activation(gates[:, :width])


def char_grid(word_ids, char_table, masked_weight, bias_row, valid):
    vocab = jnp.arange(char_table.shape[0], dtype=jnp.int32)
    onehot = (word_ids[..., None] == vocab).astype(jnp.bfloat16)
    embedded = jnp.einsum(
        "wpv,vd->wpd", onehot, char_table, preferred_element_type=jnp.float32
    ).astype(jnp.bfloat16)
    letters = word_ids.shape[1]
    padded = jnp.pad(embedded, ((0, 0), (0, KW - 1), (0, 0)))
    patches = jnp.concatenate(
        [padded[:, shift_tap : shift_tap + letters, :] for shift_tap in range(KW)], axis=2
    )
    grid = (
        jnp.einsum("wpk,kc->wpc", patches, masked_weight, preferred_element_type=jnp.float32)
        + bias_row
    )
    grid = jnp.where(valid, grid, -1e30)
    row_top = jnp.max(grid, axis=1, keepdims=True)
    log_total = row_top[:, 0, :] + jnp.log(jnp.sum(jnp.exp(grid - row_top), axis=1))
    return (onehot, patches, grid, log_total)


def low_dot(left, right):
    return jnp.dot(left, right, preferred_element_type=jnp.float32)


def dot_tn(left, right):
    return lax.dot_general(
        left, right, (((0,), (0,)), ((), ())), preferred_element_type=jnp.float32
    )


def dot_nt(left, right):
    return lax.dot_general(
        left, right, (((1,), (1,)), ((), ())), preferred_element_type=jnp.float32
    )


def per_device(
    chars,
    lengths,
    char_table,
    conv_weight,
    conv_bias,
    highway_weight,
    highway_bias,
    proj_weight,
    proj_bias,
    position,
    norm_gain,
    norm_bias,
    query_key_value_weight,
    attention_output_weight,
    feedforward_input_weight,
    feedforward_input_bias,
    feedforward_output_weight,
    cotangent,
):
    parts = lax.axis_size("filt")
    slices = lax.axis_size("dp")
    part = lax.axis_index("filt")
    slot = lax.axis_index("dp")
    seqs, quarter, dmodel = cotangent.shape
    full_len = chars.shape[1]
    letters = chars.shape[2]
    words = seqs * full_len
    tokens = seqs * quarter
    filters = conv_weight.shape[1]
    heads = dmodel // HD // parts
    width = heads * HD
    hidden_units = feedforward_output_weight.shape[0] * slices
    unit_rows = feedforward_output_weight.shape[0] // parts
    units = hidden_units // parts

    def own_columns(array, blocks):
        rows = array.shape[0]
        split = array.reshape(rows, blocks, parts, -1)
        return lax.dynamic_index_in_dim(split, part, 2, keepdims=False).reshape(rows, -1)

    def gather_rows(array):
        return lax.all_gather(array, "dp", axis=0, tiled=True)

    def to_rows(array):
        return lax.all_to_all(array, "filt", split_axis=0, concat_axis=1, tiled=True)

    def to_columns(array):
        return lax.all_to_all(array, "filt", split_axis=1, concat_axis=0, tiled=True)

    highway_own = gather_rows(own_columns(highway_weight[0], 2))
    small = jnp.concatenate(
        [
            highway_bias.reshape(-1),
            proj_bias,
            norm_gain.reshape(-1),
            norm_bias.reshape(-1),
            feedforward_input_bias,
        ]
    )
    small = lax.all_gather(small, "dp", axis=0, tiled=False)
    proj_own = to_rows(gather_rows(own_columns(proj_weight, 1)))
    qkv_own = gather_rows(own_columns(query_key_value_weight, 3))
    out_own = to_rows(gather_rows(own_columns(attention_output_weight, 1)))
    inner_own = gather_rows(own_columns(feedforward_input_weight, slices))
    outer_own = gather_rows(
        lax.dynamic_slice_in_dim(feedforward_output_weight, part * unit_rows, unit_rows, 0)
    )
    small = small.astype(jnp.float32)
    hb, pb, nd = highway_bias.shape[1], proj_bias.shape[0], norm_gain.shape[1]
    ib = feedforward_input_bias.shape[0]
    cuts = [hb, hb + pb, hb + pb + 3 * nd, hb + pb + 6 * nd]
    highway_b, proj_b, gain, shift, inner_b = jnp.split(small, cuts, axis=1)
    highway_b_own = own_columns(highway_b.reshape(1, -1), 2)
    proj_b = proj_b.reshape(-1)
    gain = gain.reshape(slices, 3, nd).transpose(1, 0, 2).reshape(3, dmodel)
    shift = shift.reshape(slices, 3, nd).transpose(1, 0, 2).reshape(3, dmodel)
    inner_b_own = own_columns(inner_b.reshape(1, -1), slices)

    def gather_tokens(array):
        array = array.reshape(seqs, quarter, -1)
        return lax.all_gather(array, "filt", axis=1, tiled=True).reshape(words, -1)

    def scatter_tokens(array):
        array = array.astype(jnp.bfloat16).reshape(seqs, full_len, -1)
        array = lax.psum_scatter(array, "filt", scatter_dimension=1, tiled=True)
        return array.reshape(tokens, -1).astype(jnp.float32)

    offset = part * filters
    word_ids = chars.reshape(words, letters)
    channels = offset + jnp.arange(filters, dtype=jnp.int32)
    widths = channel_widths(channels)
    tap_index = jnp.arange(conv_weight.shape[0], dtype=jnp.int32) // char_table.shape[1]
    tap_keep = tap_index[:, None] < widths[None, :]
    masked_weight = jnp.where(tap_keep, conv_weight, 0)
    valid = jnp.arange(letters, dtype=jnp.int32)[:, None] <= letters - widths[None, :]
    counts = (letters - widths + 1).astype(jnp.float32)
    bias_row = conv_bias.astype(jnp.float32)
    block_rows = math.gcd(words, 128)
    block_count = words // block_rows
    id_blocks = word_ids.reshape(block_count, block_rows, letters)

    def forward_block(carried, block_ids):
        onehot, patches, grid, log_total = char_grid(
            block_ids, char_table, masked_weight, bias_row, valid
        )
        return (
            carried,
            exact_gaussian_activation(log_total - jnp.log(counts)).astype(jnp.bfloat16),
        )

    unused, acts = lax.scan(forward_block, jnp.zeros((), jnp.float32), id_blocks)
    acts = acts.reshape(words, filters)
    features = lax.all_gather(acts, "filt", axis=1, tiled=True)
    gates = low_dot(features, highway_own) + highway_b_own
    feature_own = acts.astype(jnp.float32)
    hidden_low = highway_mix(feature_own, gates).astype(jnp.bfloat16)
    projected = scatter_tokens(low_dot(hidden_low, proj_own)) + proj_b
    summed = (projected.reshape(seqs, quarter, dmodel) + position.astype(jnp.float32)).reshape(
        tokens, dmodel
    )
    first_operand, norm_zero_pull = jax.vjp(layer_norm, summed, gain[0], shift[0])
    first_low = gather_tokens(first_operand.astype(jnp.bfloat16))
    packed = low_dot(first_low, qkv_own).astype(jnp.bfloat16)
    queries, keys, values = (
        packed[:, block * width : (block + 1) * width].reshape(seqs, full_len, heads, HD)
        for block in range(3)
    )
    key_ok = jnp.arange(full_len, dtype=jnp.int32)[None, :] < lengths[:, None]
    scale = HD ** (-0.5)
    scores = (
        jnp.einsum("sqhd,skhd->shqk", queries, keys, preferred_element_type=jnp.float32) * scale
    )
    scores = jnp.where(key_ok[:, None, None, :], scores, -1e30)
    row_top = jnp.max(scores, axis=-1, keepdims=True)
    log_total = row_top + jnp.log(jnp.sum(jnp.exp(scores - row_top), axis=-1, keepdims=True))
    probs = jnp.exp(scores - log_total)
    probs_low = probs.astype(jnp.bfloat16)
    attended = (
        jnp.einsum("shqk,skhd->sqhd", probs_low, values, preferred_element_type=jnp.float32)
        .astype(jnp.bfloat16)
        .reshape(words, width)
    )
    mixed = scatter_tokens(low_dot(attended, out_own))
    second_operand, norm_one_pull = jax.vjp(layer_norm, first_operand + mixed, gain[1], shift[1])
    second_low = gather_tokens(second_operand.astype(jnp.bfloat16))
    inner = low_dot(second_low, inner_own) + inner_b_own
    active = exact_gaussian_activation(inner).astype(jnp.bfloat16)
    outer = scatter_tokens(low_dot(active, outer_own))
    top_out, norm_two_pull = jax.vjp(layer_norm, second_operand + outer, gain[2], shift[2])
    encoded = top_out.astype(jnp.bfloat16).reshape(seqs, quarter, dmodel)
    upstream = cotangent.reshape(tokens, dmodel).astype(jnp.float32)
    d_res_two, d_gain_two, d_shift_two = norm_two_pull(upstream)
    d_outer = gather_tokens(d_res_two.astype(jnp.bfloat16))

    def reduce_rows(array):
        return lax.psum_scatter(
            array.astype(jnp.bfloat16), "dp", scatter_dimension=0, tiled=True
        )

    grad_outer = reduce_rows(dot_tn(active, d_outer))
    d_active = dot_nt(d_outer, outer_own)
    d_inner = gelu_back(inner, d_active).astype(jnp.bfloat16)
    grad_inner = reduce_rows(dot_tn(second_low, d_inner))
    grad_inner_b = jnp.sum(d_inner.astype(jnp.float32), axis=0)
    d_second = d_res_two + scatter_tokens(dot_nt(d_inner, inner_own))
    d_res_one, d_gain_one, d_shift_one = norm_one_pull(d_second)
    d_mixed = gather_tokens(d_res_one.astype(jnp.bfloat16))
    grad_out = reduce_rows(to_columns(dot_tn(attended, d_mixed).astype(jnp.bfloat16)))
    d_attended = dot_nt(d_mixed, out_own).astype(jnp.bfloat16)
    d_attended = d_attended.reshape(seqs, full_len, heads, HD)
    d_values = jnp.einsum(
        "shqk,sqhd->skhd", probs_low, d_attended, preferred_element_type=jnp.float32
    )
    d_probs = jnp.einsum(
        "sqhd,skhd->shqk", d_attended, values, preferred_element_type=jnp.float32
    )
    row_inner = jnp.sum(d_probs * probs, axis=-1, keepdims=True)
    d_scores = (probs * (d_probs - row_inner)).astype(jnp.bfloat16)
    d_queries = (
        jnp.einsum("shqk,skhd->sqhd", d_scores, keys, preferred_element_type=jnp.float32) * scale
    )
    d_keys = (
        jnp.einsum("shqk,sqhd->skhd", d_scores, queries, preferred_element_type=jnp.float32) * scale
    )
    d_packed = jnp.concatenate(
        [item.reshape(words, width) for item in (d_queries, d_keys, d_values)], axis=1
    ).astype(jnp.bfloat16)
    grad_qkv = reduce_rows(dot_tn(first_low, d_packed))
    d_first = d_res_one + scatter_tokens(dot_nt(d_packed, qkv_own))
    d_summed, d_gain_zero, d_shift_zero = norm_zero_pull(d_first)
    grad_pos = jnp.sum(d_summed.reshape(seqs, quarter, dmodel), axis=0)
    d_projected_own = d_summed.astype(jnp.bfloat16)
    d_projected = gather_tokens(d_projected_own)
    grad_proj_b = jnp.sum(d_projected_own.astype(jnp.float32), axis=0)
    grad_proj = reduce_rows(to_columns(dot_tn(hidden_low, d_projected).astype(jnp.bfloat16)))
    d_hidden = dot_nt(d_projected, proj_own)
    d_in, d_gates = jax.vjp(highway_mix, feature_own, gates)[1](d_hidden)
    d_gates = d_gates.astype(jnp.bfloat16)
    grad_highway = reduce_rows(dot_tn(features, d_gates))
    grad_highway_b = jnp.sum(d_gates.astype(jnp.float32), axis=0)
    d_mixed_in = lax.psum_scatter(
        dot_nt(d_gates, highway_own).astype(jnp.bfloat16), "filt", scatter_dimension=1, tiled=True
    )
    d_features = (d_in + d_mixed_in.astype(jnp.float32)).astype(jnp.bfloat16)
    d_blocks = d_features.reshape(block_count, block_rows, -1)
    depth = char_table.shape[1]

    def backward_block(totals, item):
        block_ids, block_grad = item
        onehot, patches, grid, log_total = char_grid(
            block_ids, char_table, masked_weight, bias_row, valid
        )
        d_pooled = gelu_back(log_total - jnp.log(counts), block_grad.astype(jnp.float32))
        position_weights = jnp.exp(grid - log_total[:, None, :])
        d_grid = (position_weights * d_pooled[:, None, :]).astype(jnp.bfloat16)
        grad_weight = totals[0] + jnp.einsum(
            "wpk,wpc->kc", patches, d_grid, preferred_element_type=jnp.float32
        )
        grad_bias = totals[1] + jnp.sum(d_grid.astype(jnp.float32), axis=(0, 1))
        d_patch = jnp.einsum(
            "wpc,kc->wpk", d_grid, masked_weight, preferred_element_type=jnp.float32
        )
        pieces = [
            jnp.pad(
                d_patch[:, :, shift_tap * depth : (shift_tap + 1) * depth],
                ((0, 0), (shift_tap, KW - 1 - shift_tap), (0, 0)),
            )
            for shift_tap in range(KW)
        ]
        d_embedded = reduce(jnp.add, pieces)[:, :letters, :]
        grad_table = totals[2] + jnp.einsum(
            "wpv,wpd->vd", onehot.astype(jnp.float32), d_embedded, precision=lax.Precision.HIGHEST
        )
        return ((grad_weight, grad_bias, grad_table), None)

    start = (
        jnp.zeros(masked_weight.shape, jnp.float32),
        jnp.zeros(bias_row.shape, jnp.float32),
        jnp.zeros(char_table.shape, jnp.float32),
    )
    char_totals, unused_rows = lax.scan(backward_block, start, (id_blocks, d_blocks))
    conv_grad_w = jnp.where(tap_keep, char_totals[0], 0.0)
    conv_grad_w, conv_grad_b, grad_pos = lax.psum((conv_grad_w, char_totals[1], grad_pos), "dp")

    def place_columns(own, blocks):
        piece = own.reshape(blocks, 1, -1)
        whole = jnp.zeros((blocks, parts, piece.shape[2]), own.dtype)
        return lax.dynamic_update_slice_in_dim(whole, piece, part, 1).reshape(-1)

    d_gain = jnp.stack([d_gain_zero, d_gain_one, d_gain_two])
    d_shift = jnp.stack([d_shift_zero, d_shift_one, d_shift_two])
    pieces = [
        place_columns(grad_highway_b, 2).reshape(slices, -1),
        grad_proj_b.reshape(slices, -1),
        d_gain.reshape(3, slices, nd).transpose(1, 0, 2).reshape(slices, -1),
        d_shift.reshape(3, slices, nd).transpose(1, 0, 2).reshape(slices, -1),
        place_columns(grad_inner_b, slices).reshape(slices, -1),
    ]
    rows = jnp.concatenate(pieces, axis=1)
    row_size = rows.shape[1]
    table_size = char_totals[2].size
    sums = lax.psum(
        jnp.concatenate([rows.reshape(-1), char_totals[2].reshape(-1)]), ("dp", "filt")
    )
    g_table = sums[rows.size :].reshape(char_totals[2].shape)
    own = lax.dynamic_slice_in_dim(sums, slot * row_size, row_size, 0)
    g_highway_b, g_proj_b, g_gain, g_shift, g_inner_b = jnp.split(own, cuts)

    def join_columns(array, blocks):
        rows_here = array.shape[0]
        whole = lax.all_gather(array, "filt", axis=0, tiled=False)
        whole = whole.reshape(parts, rows_here, blocks, -1).transpose(1, 2, 0, 3)
        return whole.reshape(rows_here, -1).astype(jnp.float32)

    g_outer = lax.all_gather(grad_outer, "filt", axis=0, tiled=True).astype(jnp.float32)
    g_inner = join_columns(grad_inner, slices)
    g_out = join_columns(grad_out, 1)
    g_qkv = join_columns(grad_qkv, 3)
    g_proj = join_columns(grad_proj, 1)
    g_highway = join_columns(grad_highway, 2)
    return (
        encoded,
        g_table,
        conv_grad_w,
        conv_grad_b,
        g_highway[None],
        g_highway_b[None],
        g_proj,
        g_proj_b,
        grad_pos,
        g_gain.reshape(3, nd),
        g_shift.reshape(3, nd),
        g_qkv,
        g_out,
        g_inner,
        g_inner_b,
        g_outer,
    )


def solution(mesh):
    return jax.shard_map(
        per_device,
        mesh=mesh,
        in_specs=(
            P("dp", None, None),
            P("dp"),
            P(),
            P(None, "filt"),
            P("filt"),
            P(None, "dp", None),
            P(None, "dp"),
            P("dp", None),
            P("dp"),
            P("filt", None),
            P(None, "dp"),
            P(None, "dp"),
            P("dp", None),
            P("dp", None),
            P("dp", None),
            P("dp"),
            P("dp", None),
            P("dp", "filt", None),
        ),
        out_specs=(
            P("dp", "filt", None),
            P(),
            P(None, "filt"),
            P("filt"),
            P(None, "dp", None),
            P(None, "dp"),
            P("dp", None),
            P("dp"),
            P("filt", None),
            P(None, "dp"),
            P(None, "dp"),
            P("dp", None),
            P("dp", None),
            P("dp", None),
            P("dp"),
            P("dp", None),
        ),
        check_vma=False,
    )
```

time: 2240 us -> 1200 us (0.54)
  waiting for transfers between devices: 1670 us -> 582 us
  blocking collectives: 174 us -> 250 us
  matrix products: 163 us -> 122 us
  local copies, waits for them, and re-layouts: 68.9 us -> 96.9 us
    reduce_scatter x6 -> x12, waiting for transfers between devices: 1110 us -> 314 us  [the longest x6 232 us: reduce_rows(): lax.psum_scatter(array.astype(jnp.bfloat16), 'dp', scatter_dimension=0, t...]
    all_gather x6 -> x5, waiting for transfers between devices: 352 us -> 104 us  [the longest x3 85.5 us: gather_rows(): return lax.all_gather(array, 'dp', axis=0, tiled=True)]
    unnamed x24 -> x19, waiting for transfers between devices: 104 us -> 0.79 us
    all_gather x6 -> x13, blocking collectives: 108 us -> 176 us  [the longest x3 98.8 us: gather_rows(): return lax.all_gather(array, 'dp', axis=0, tiled=True)]
    psum x2, waiting for transfers between devices: 108 us -> 154 us  [the longest x1 94.8 us: per_device(): lax.psum(jnp.concatenate([rows.reshape(-1), char_totals[2].reshape(-1)]),...]
    dot_general x22, matrix products: 93.5 us -> 52.8 us  [the longest x6 19.1 us: low_dot(): return jnp.dot(left, right, preferred_element_type=jnp.float32)]
    convert_element_type x3 -> x16, local copies, waits for them, and re-layouts: 1.91 us -> 32.8 us  [the longest x14 31.5 us: join_columns(): return whole.reshape(rows_here, -1).astype(jnp.float32)]
    psum x2 -> x1, blocking collectives: 47.2 us -> 20.2 us  [per_device(): lax.psum((conv_grad_w, char_totals[1], grad_pos), 'dp')]
  transfers between devices with their start and end apart: 21 -> 22, of which waited for: 17 -> 16; matrix products, arithmetic and copies ran while one was open for 13% -> 19% of each run, Pallas kernels for 0% -> 0%
where the time goes in v1:
time: 1200 us; the launch traced here: 1190 us
  waiting for transfers between devices  582 us (48%)
  blocking collectives  250 us (21%)
  matrix products  122 us (10%)
  other arithmetic  105 us (9%)
  local copies, waits for them, and re-layouts  96.9 us (8%)
  between operations  16.8 us (1%)
  starting transfers between devices  12.6 us (1%)
    reduce_scatter x6, waiting for transfers between devices, reduce_rows(): lax.psum_scatter(array.astype(jnp.bfloat16), 'dp', scatter_dimension=0, t...  232 us
    all_gather x3, blocking collectives, gather_rows(): return lax.all_gather(array, 'dp', axis=0, tiled=True)  98.8 us
    psum x1, waiting for transfers between devices, per_device(): lax.psum(jnp.concatenate([rows.reshape(-1), char_totals[2].reshape(-1)]),...  94.8 us
    all_gather x3, waiting for transfers between devices, gather_rows(): return lax.all_gather(array, 'dp', axis=0, tiled=True)  85.5 us
    reduce_scatter x5, waiting for transfers between devices, scatter_tokens(): array = lax.psum_scatter(array, 'filt', scatter_dimension=1, tiled=True)  82 us
    psum x1, waiting for transfers between devices, per_device(): lax.psum((conv_grad_w, char_totals[1], grad_pos), 'dp')  59 us
    all_gather x5, blocking collectives, gather_tokens(): return lax.all_gather(array, 'filt', axis=1, tiled=True).reshape(words, -1)  42.1 us
    reduce_sum x4, other arithmetic, backward_block(): grad_bias = totals[1] + jnp.sum(d_grid.astype(jnp.float32), axis=(0, 1))  41.1 us
  transfers between devices with their start and end apart: 22, of which 16 were waited for; matrix products, arithmetic and copies ran while one was open for 19% of the time, Pallas kernels for 0%

profile of v1, /device:TPU:0, one launch (start us, length us, event | category | flops | bytes accessed | tf_op | source)
XLA Modules:
  0.0 1186.4 jit_solution(14059333220793541380)
XLA Ops:
  10.0 33.9 %while.30 = (s32[]{:T(128)}, bf16[4,128,512]{2,1,0:T(8,128)(2,1)}, s32[4,128,50]{1,2,0:T(8,128)S(1)}, bf16[262,16]{0,1:T(8,128)(2,1)}, bf16[112,512]{1,0:T(8,128...) while((s32[]{:T(128)}, bf16[4,128,512]{2,1,0:T(8,128)(2,1)}, ...), condition=%wide.region_3.4_spmd.clone, body=%wide.region_0.3_spmd.clone.sunk | while | flops 816673792 | bytes 32244016 | solution.py:192
  48.6 33.9 %all-gather.1 = bf16[2048,1,1,192]{0,3,2,1:T(8,128)(2,1)S(1)} all-gather(bf16[256,1,1,192]{0,3,2,1:T(8,128)(2,1)S(1)} %constant_dynamic-slice_fusion.3), channel_id=3, replica_groups=mesh['dp'=8,'filt'=4] {'dp'}, dimensions={0}, use_global_device_ids=true | all-gather | bytes 884736 | tf_op jit(solution)/shard_map/all_gather | solution.py:123
  89.5 39.6 %all-reduce.11 = bf16[12544]{0:T(1024)(128)(2,1)S(1)} all-reduce(bf16[12544]{0:T(1024)(128)(2,1)S(1)} %dynamic-update-slice), channel_id=2, replica_groups=mesh['dp'=8,'filt'=4] {'dp'}, use_global_device_ids=true, to_apply=%add.11 | all-reduce | flops 12544 | bytes 50176
  129.3 18.6 %all-gather.17.cloned.1.call-done = bf16[2048,1024]{0,1:T(8,128)(2,1)} async-done(((bf16[256,1024]{0,1:T(8,128)(2,1)}), bf16[2048,1024]{0,1:T(8,128)(2,1)}) %all-gather.17.cloned.1.call-update) | async-done | bytes 4194320 | tf_op jit(solution)/shard_map/all_gather | solution.py:123
  159.8 32.1 %all-gather.3 = bf16[768,1,1,192]{3,2,1,0:T(2,128)(2,1)S(1)} all-gather(bf16[96,1,1,192]{3,2,1,0:T(2,128)(2,1)S(1)} %constant_dynamic-slice_fusion.1), channel_id=5, replica_groups=mesh['dp'=8,'filt'=4] {'dp'}, dimensions={0}, use_global_device_ids=true | all-gather | bytes 331776 | tf_op jit(solution)/shard_map/all_gather | solution.py:123
  199.4 32.9 %all_gather.81 = bf16[768,576]{1,0:T(8,128)(2,1)S(1)} all-gather(bf16[96,576]{1,0:T(8,128)(2,1)S(1)} %copy.153), channel_id=1, replica_groups=mesh['dp'=8,'filt'=4] {'dp'}, dimensions={0}, use_global_device_ids=true | all-gather | bytes 995328 | tf_op jit(solution)/shard_map/all_gather | solution.py:123
  235.9 8.9 all-gather.2
  258.5 12.6 %reduce-scatter.19.cloned.1.call-done = bf16[1,128,768]{2,1,0:T(8,128)(2,1)} async-done(((bf16[1,512,768]{2,1,0:T(8,128)(2,1)}), bf16[1,128,768]{2,1,0:T(8,128)(2,1)}) %reduce-scatter.19.cloned.1.call-update) | async-done | bytes 196624 | tf_op jit(solution)/shard_map/reduce_scatter | solution.py:166
  274.5 8.6 all_gather.83
  283.1 31.8 %all-gather.19.cloned.1.call-done = bf16[768,768]{1,0:T(8,128)(2,1)} async-done(((bf16[96,768]{1,0:T(8,128)(2,1)}), bf16[768,768]{1,0:T(8,128)(2,1)}) %all-gather.19.cloned.1.call-update) | async-done | bytes 1179664 | tf_op jit(solution)/shard_map/all_gather | solution.py:123
  322.2 35.2 %all-gather.21.cloned.1.call-done = bf16[768,768]{1,0:T(8,128)(2,1)} async-done(((bf16[96,768]{1,0:T(8,128)(2,1)}), bf16[768,768]{1,0:T(8,128)(2,1)}) %all-gather.21.cloned.1.call-update) | async-done | bytes 1179664 | tf_op jit(solution)/shard_map/all_gather | solution.py:123
  360.7 22.1 %reduce-scatter.21.cloned.1.call-done = bf16[1,128,768]{2,1,0:T(8,128)(2,1)} async-done(((bf16[1,512,768]{2,1,0:T(8,128)(2,1)}), bf16[1,128,768]{2,1,0:T(8,128)(2,1)}) %reduce-scatter.21.cloned.1.call-update) | async-done | bytes 196624 | tf_op jit(solution)/shard_map/reduce_scatter | solution.py:166
  386.1 8.2 all_gather.86
  400.7 23.5 %reduce-scatter.23.cloned.1.call-done = bf16[1,128,768]{2,1,0:T(8,128)(2,1)} async-done(((bf16[1,512,768]{2,1,0:T(8,128)(2,1)}), bf16[1,128,768]{2,1,0:T(8,128)(2,1)}) %reduce-scatter.23.cloned.1.call-update) | async-done | bytes 196624 | tf_op jit(solution)/shard_map/reduce_scatter | solution.py:166
  445.5 23.8 %reduce-scatter.25.cloned.1.call-done = bf16[1,128,768]{2,1,0:T(8,128)(2,1)} async-done(((bf16[1,512,768]{2,1,0:T(8,128)(2,1)}), bf16[1,128,768]{2,1,0:T(8,128)(2,1)}) %reduce-scatter.25.cloned.1.call-update) | async-done | bytes 196624 | tf_op jit(solution)/shard_map/reduce_scatter | solution.py:166
  473.0 8.2 all_gather.88
  502.7 14.1 %all_to_all.76 = bf16[192,4,192]{0,2,1:T(8,128)(2,1)S(1)} all-to-all(bf16[192,4,192]{0,2,1:T(8,128)(2,1)S(1)} %bitcast.348), channel_id=1, replica_groups=mesh['dp'=8,'filt'=4] {'filt'}, dimensions={1} | all-to-all | bytes 589824 | tf_op jit(solution)/shard_map/all_to_all | solution.py:129
  530.9 8.9 all-to-all-done.2
  544.6 127.7 %while.31 = (s32[]{:T(128)}, f32[112,512]{1,0:T(8,128)S(1)}, f32[512]{0:T(512)S(1)}, f32[262,16]{0,1:T(8,128)S(1)}, s32[4,128,50]{1,2,0:T(8,128)}, /*index=5*/bf...) while((s32[]{:T(128)}, f32[112,512]{1,0:T(8,128)S(1)}, ...), condition=%wide.region_38.39_spmd.clone, body=%wide.region_34.38_spmd.clone.sunk | while | flops 2619329792 | bytes 151665840 | solution.py:322
  555.9 10.4 convert_reduce_fusion.6
  587.9 10.3 convert_reduce_fusion.6
  619.6 10.2 convert_reduce_fusion.6
  651.3 10.2 convert_reduce_fusion.6
  673.9 10.9 reduce-scatter.35.cloned.1.call-done
  694.4 57.9 %reduce-scatter.33.cloned.1.call-done = bf16[96,768]{1,0:T(8,128)(2,1)} async-done(((bf16[768,768]{1,0:T(8,128)(2,1)}), bf16[96,768]{1,0:T(8,128)(2,1)}) %reduce-scatter.33.cloned.1.call-update) | async-done | bytes 147472 | tf_op jit(solution)/shard_map/reduce_scatter | solution.py:237
  766.5 49.7 %reduce-scatter.39.cloned.1.call-done = bf16[96,192]{1,0:T(8,128)(2,1)} async-done(((bf16[768,192]{1,0:T(8,128)(2,1)}), bf16[96,192]{1,0:T(8,128)(2,1)}) %reduce-scatter.39.cloned.1.call-update) | async-done | bytes 36880 | tf_op jit(solution)/shard_map/reduce_scatter | solution.py:237
  823.6 58.6 %reduce-scatter.37.cloned.1.call-done = bf16[96,576]{1,0:T(8,128)(2,1)} async-done(((bf16[768,576]{1,0:T(8,128)(2,1)}), bf16[96,576]{1,0:T(8,128)(2,1)}) %reduce-scatter.37.cloned.1.call-update) | async-done | bytes 110608 | tf_op jit(solution)/shard_map/reduce_scatter | solution.py:237
  893.2 54.9 %reduce-scatter.31.cloned.1.call-done = bf16[256,192]{0,1:T(8,128)(2,1)} async-done(((bf16[2048,192]{0,1:T(8,128)(2,1)}), bf16[256,192]{0,1:T(8,128)(2,1)}) %reduce-scatter.31.cloned.1.call-update) | async-done | bytes 98320 | tf_op jit(solution)/shard_map/reduce_scatter | solution.py:237
  956.4 20.2 %psum.30 = f32[512]{0:T(512)} all-reduce(f32[512]{0:T(512)S(1)} %get-tuple-element.264), channel_id=1, replica_groups=mesh['dp'=8,'filt'=4] {'dp'}, use_global_device_ids=true, to_apply=%region_41.42 | all-reduce | flops 512 | bytes 4096 | tf_op jit(solution)/shard_map/psum | solution.py:324
  976.6 94.8 %all-reduce.16.cloned.1.call-done = f32[16736]{0:T(1024)} async-done(((f32[16736]{0:T(1024)}), f32[16736]{0:T(1024)}) %all-reduce.16.cloned.1.call-update) | async-done | bytes 66960 | tf_op jit(solution)/shard_map/psum | solution.py:343
  1079.1 18.7 %all-gather.23.cloned.1.call-done = bf16[1024,1024]{1,0:T(8,128)(2,1)} async-done(((bf16[256,1024]{1,0:T(8,128)(2,1)}), bf16[1024,1024]{1,0:T(8,128)(2,1)}) %all-gather.23.cloned.1.call-update) | async-done | bytes 2097168 | tf_op jit(solution)/shard_map/all_gather | solution.py:352
  1117.2 59.0 %all-reduce.18.cloned.1.call-done = (f32[112,512]{1,0:T(8,128)}, f32[128,768]{1,0:T(8,128)}) async-done(((f32[112,512]{1,0:T(8,128)}, f32[128,768]{1,0:T(8,128)}), (f32[112,512]{1,0:T(8,128)}, f32[128,768]{1,0:T(8,128)})) %all-reduce.18.cloned.1.call-update) | async-done | bytes 622608 | tf_op jit(solution)/shard_map/psum | solution.py:324
  (539 shorter events, 339.4 us)
Async XLA Ops:
  7.2 250.2 %copy-start = (bf16[384,768]{1,0:T(8,128)(2,1)S(1)}, bf16[384,768]{1,0:T(8,128)(2,1)}, u32[]{:S(2)}) copy-start(bf16[384,768]{1,0:T(8,128)(2,1)} %param.38) | copy-start | bytes 1769476
  7.2 122.1 %all-gather.15.cloned.1.call-start = ((), (), s32[]{:S(2)}) async-start(), calls=%async_computation.16 | async-start | bytes 2621440 | tf_op jit(solution)/shard_map/all_gather | solution.py:194
  43.9 104.0 %all-gather.17.cloned.1.call-start = ((), (), s32[]{:S(2)}) async-start(), calls=%async_computation.17 | async-start | bytes 4718592 | tf_op jit(solution)/shard_map/all_gather | solution.py:123
  84.1 73.8 %all-to-all-start = ((bf16[4,512,192]{1,2,0:T(8,128)(2,1)}), bf16[4,512,192]{1,2,0:T(8,128)(2,1)S(1)}, u32[]{:S(2)}, u32[]{:S(2)}) async-start(bf16[4,512,192]{1,2,0:T(8,128)(2,1)} %copy.151), calls=%async_computation | async-start | bytes 1572864 | tf_op jit(solution)/shard_map/all_to_all | solution.py:126
  87.6 144.7 %reduce-scatter.17.cloned.1.call-start = ((), (), s32[]{:S(2)}) async-start(), calls=%async_computation.18 | async-start | bytes 983040 | tf_op jit(solution)/shard_map/reduce_scatter | solution.py:166
  192.9 56.3 %all-to-all-start.1 = ((bf16[4,192,192]{1,2,0:T(8,128)(2,1)}), bf16[4,192,192]{1,2,0:T(8,128)(2,1)S(1)}, u32[]{:S(2)}, u32[]{:S(2)}) async-start(bf16[4,192,192]{1,2,0:T(8,128)(2,1)} %copy.156), calls=%async_computation.2 | async-start | bytes 786432 | tf_op jit(solution)/shard_map/all_to_all | solution.py:126
  196.3 74.8 %reduce-scatter.19.cloned.1.call-start = ((), (), s32[]{:S(2)}) async-start(), calls=%async_computation.19 | async-start | bytes 983040 | tf_op jit(solution)/shard_map/reduce_scatter | solution.py:166
  198.1 34.2 %copy-start.5 = (bf16[128,768]{1,0:T(8,128)(2,1)S(1)}, bf16[128,768]{1,0:T(8,128)(2,1)}, u32[]{:S(2)}) copy-start(bf16[128,768]{1,0:T(8,128)(2,1)} %param.31) | copy-start | bytes 589828
  199.4 47.8 %copy-start.63 = (pred[512]{0:T(512)(128)(4,1)}, pred[512]{0:T(512)(128)(4,1)S(1)}, u32[]{:S(2)}) copy-start(pred[512]{0:T(512)(128)(4,1)S(1)} %iota_compare_fusion.15) | copy-start | bytes 1540
  233.6 38.9 %copy-start.53 = (f32[128]{0:T(128)}, f32[128]{0:T(128)S(1)}, u32[]{:S(2)}) copy-start(f32[128]{0:T(128)S(1)} %broadcast_multiply_fusion.2) | copy-start | bytes 1540
  234.8 37.8 %copy-start.55 = (f32[128]{0:T(128)}, f32[128]{0:T(128)S(1)}, u32[]{:S(2)}) copy-start(f32[128]{0:T(128)S(1)} %fusion.144) | copy-start | bytes 1540
  250.5 64.4 %all-gather.19.cloned.1.call-start = ((), (), s32[]{:S(2)}) async-start(), calls=%async_computation.20 | async-start | bytes 1327104 | tf_op jit(solution)/shard_map/all_gather | solution.py:123
  257.3 100.0 %all-gather.21.cloned.1.call-start = ((), (), s32[]{:S(2)}) async-start(), calls=%async_computation.21 | async-start | bytes 1327104 | tf_op jit(solution)/shard_map/all_gather | solution.py:123
  258.1 124.6 %reduce-scatter.21.cloned.1.call-start = ((), (), s32[]{:S(2)}) async-start(), calls=%async_computation.22 | async-start | bytes 983040 | tf_op jit(solution)/shard_map/reduce_scatter | solution.py:166
  360.6 63.7 %reduce-scatter.23.cloned.1.call-start = ((), (), s32[]{:S(2)}) async-start(), calls=%async_computation.23 | async-start | bytes 983040 | tf_op jit(solution)/shard_map/reduce_scatter | solution.py:166
  400.4 68.8 %reduce-scatter.25.cloned.1.call-start = ((), (), s32[]{:S(2)}) async-start(), calls=%async_computation.24 | async-start | bytes 983040 | tf_op jit(solution)/shard_map/reduce_scatter | solution.py:166
  443.6 25.6 %copy-start.54 = (f32[128]{0:T(128)S(1)}, f32[128]{0:T(128)}, u32[]{:S(2)}) copy-start(f32[128]{0:T(128)} %copy-done.53) | copy-start | bytes 1540
  443.6 25.6 %copy-start.56 = (f32[128]{0:T(128)S(1)}, f32[128]{0:T(128)}, u32[]{:S(2)}) copy-start(f32[128]{0:T(128)} %copy-done.55) | copy-start | bytes 1540
  445.4 25.2 %copy-start.73 = (f32[128]{0:T(128)S(1)}, f32[128]{0:T(128)}, u32[]{:S(2)}) copy-start(f32[128]{0:T(128)} %copy-done.72) | copy-start | bytes 1540
  445.4 26.6 %copy-start.25 = (f32[1,128,768]{2,1,0:T(8,128)S(1)}, f32[1,128,768]{2,1,0:T(8,128)}, u32[]{:S(2)}) copy-start(f32[1,128,768]{2,1,0:T(8,128)} %get-tuple-element.568) | copy-start | bytes 1179652
  445.4 96.6 %reduce-scatter.27.cloned.1.call-start = ((), (), s32[]{:S(2)}) async-start(), calls=%async_computation.25 | async-start | bytes 2621440 | tf_op jit(solution)/shard_map/reduce_scatter | solution.py:282
  488.2 185.1 %reduce-scatter.29.cloned.1.call-start = ((), (), s32[]{:S(2)}) async-start(), calls=%async_computation.27 | async-start | bytes 4718592 | tf_op jit(solution)/shard_map/reduce_scatter | solution.py:237
  494.6 190.2 %reduce-scatter.35.cloned.1.call-start = ((), (), s32[]{:S(2)}) async-start(), calls=%async_computation.30 | async-start | bytes 1327104 | tf_op jit(solution)/shard_map/reduce_scatter | solution.py:237
  498.8 253.5 %reduce-scatter.33.cloned.1.call-start = ((), (), s32[]{:S(2)}) async-start(), calls=%async_computation.29 | async-start | bytes 1327104 | tf_op jit(solution)/shard_map/reduce_scatter | solution.py:237
  502.1 314.0 %reduce-scatter.39.cloned.1.call-start = ((), (), s32[]{:S(2)}) async-start(), calls=%async_computation.33 | async-start | bytes 442368 | tf_op jit(solution)/shard_map/reduce_scatter | solution.py:237
  517.9 364.3 %reduce-scatter.37.cloned.1.call-start = ((), (), s32[]{:S(2)}) async-start(), calls=%async_computation.32 | async-start | bytes 1105920 | tf_op jit(solution)/shard_map/reduce_scatter | solution.py:237
  523.9 15.9 %all-to-all-start.2 = ((bf16[512,4,192]{0,2,1:T(8,128)(2,1)}), bf16[512,4,192]{0,2,1:T(8,128)(2,1)}, u32[]{:S(2)}, u32[]{:S(2)}) async-start(bf16[512,4,192]{0,2,1:T(8,128)(2,1)} %bitcast.56), calls=%async_computation.9 | async-start | bytes 1572864 | tf_op jit(solution)/shard_map/all_to_all | solution.py:129
  528.1 420.0 %reduce-scatter.31.cloned.1.call-start = ((), (), s32[]{:S(2)}) async-start(), calls=%async_computation.28 | async-start | bytes 884736 | tf_op jit(solution)/shard_map/reduce_scatter | solution.py:237
  542.0 529.4 %all-reduce.16.cloned.1.call-start = ((), (), s32[]{:S(2)}) async-start(), calls=%async_computation.26 | async-start | bytes 139264 | tf_op jit(solution)/shard_map/psum | solution.py:343
  673.2 424.5 %all-gather.23.cloned.1.call-start = ((), (), s32[]{:S(2)}) async-start(), calls=%async_computation.31 | async-start | bytes 2621440 | tf_op jit(solution)/shard_map/all_gather | solution.py:352
  673.8 502.5 %all-reduce.18.cloned.1.call-start = ((), (), s32[]{:S(2)}) async-start(), calls=%async_computation.34 | async-start | bytes 1245184 | tf_op jit(solution)/shard_map/psum | solution.py:324
  1111.1 68.6 %copy-start.1 = (bf16[384,768]{1,0:T(8,128)(2,1)S(1)}, bf16[384,768]{1,0:T(8,128)(2,1)}, u32[]{:S(2)}) copy-start(bf16[384,768]{1,0:T(8,128)(2,1)} %param.38) | copy-start | bytes 1769476
  (83 other events, 452.3 us)
Sparse Core Ops, SparseCore 0:
  44.0 25.2 all-gather.14
  71.9 75.9 all-gather.16
  159.6 21.5 reduce-scatter.16
  250.6 20.5 reduce-scatter.18
  273.8 41.0 all-gather.18
  317.5 39.8 all-gather.20
  360.7 22.0 reduce-scatter.20
  400.5 23.6 reduce-scatter.22
  445.5 23.6 reduce-scatter.24
  488.4 36.0 reduce-scatter.26
  528.6 87.9 reduce-scatter.28
  620.8 63.9 reduce-scatter.34
  689.1 63.1 reduce-scatter.32
  755.7 60.3 reduce-scatter.38
  819.7 62.4 reduce-scatter.36
  885.9 62.1 reduce-scatter.30
  954.5 116.8 all-reduce.15
  1072.9 24.8 all-gather.22
  1102.8 73.4 all-reduce.17
